TPU v7x, 128 devices: a whole 4x4x4 slice. The times are simulated.
128 devices in a mesh: row: 8 (over y, core), col: 16 (over z, x).
Axes of the slice: x: 4, y: 4, z: 4, core: 2. Of those that a mesh axis runs over, the one named last changes fastest.
Arguments:
- pan_left: bfloat16 [32, 2048, 512], P('row', 'col'), may hold values from -6 to 6
- pan_right: bfloat16 [32, 2048, 512], P('row', 'col'), may hold values from -0.125 to 0.125
- inverse: bfloat16 [2048, 2048], P('col'), may hold values from -0.25 to 1.25, as said below
- rank_list: int32 [32], replicated, may hold values from 32 to 512, as said below
Outputs:
- update_right: bfloat16 [32, 32, 2048, 512], P('row', 'col')
- update_gram: bfloat16 [32, 32, 512, 512], P('row', 'col')
Inputs may be any that keep to these rules, and one draw needn't show every extreme that they name: `inverse`: lower triangular; diagonal entries lie from 0.75 to 1.25. `rank_list`: columns of a tile's factors at or beyond its rank do not count.
All inputs are finite; a program needn't handle non-finite values.
Results may differ from a plain program's by a relative error of at most 0.0065.
Values may be sent and summed in bfloat16 or wider, within the bound.
A program may use at most 128 MiB of HBM per device.

v0:
```python
import jax
import jax.numpy as jnp
from jax import lax
from jax.sharding import PartitionSpec as P


def from_root(array, axis, root):
    mine = lax.axis_index(axis) == root
    return lax.psum(jnp.where(mine, array, jnp.zeros_like(array)), axis)


def local(pan_left, pan_right, inverse, rank_list):
    tile_count = pan_right.shape[0]
    rank_width = pan_right.shape[2]
    row_count = inverse.shape[1]
    tile_total = tile_count * lax.axis_size("row")
    per_column = tile_total // lax.axis_size("col")
    my_row = lax.axis_index("row")
    my_col = lax.axis_index("col")
    full_right = lax.all_gather(pan_right, "col", axis=1, tiled=True)
    solved_slab = jnp.einsum(
        "rn,tnk->trk", inverse, full_right, preferred_element_type=jnp.float32
    ).astype(jnp.bfloat16)
    full_solved, full_left = (
        lax.all_gather(solved_slab, "col", axis=1, tiled=True),
        lax.all_gather(pan_left, "col", axis=1, tiled=True),
    )
    first_tile = my_col * per_column
    root_row = first_tile // tile_count
    local_start = first_tile % tile_count
    pick_solved = lax.dynamic_slice_in_dim(full_solved, local_start, per_column, 0)
    pick_left = lax.dynamic_slice_in_dim(full_left, local_start, per_column, 0)
    col_solved, col_left = (
        from_root(pick_solved, "row", root_row),
        from_root(pick_left, "row", root_row),
    )
    positions = jnp.arange(rank_width, dtype=jnp.int32)
    mine_ranks = lax.dynamic_slice_in_dim(rank_list, my_row * tile_count, tile_count, 0)
    their_ranks = lax.dynamic_slice_in_dim(rank_list, first_tile, per_column, 0)
    mine_live = (positions[None, :] < mine_ranks[:, None]).astype(jnp.float32)
    their_live = (positions[None, :] < their_ranks[:, None]).astype(jnp.float32)
    core = jnp.einsum("tnk,unl->tukl", full_solved, col_solved, preferred_element_type=jnp.float32)
    core = (core * mine_live[:, None, :, None] * their_live[None, :, None, :]).astype(jnp.bfloat16)
    update = jnp.einsum(
        "unl,tukl->tunk", col_left, core, preferred_element_type=jnp.float32
    ).astype(jnp.bfloat16)
    gram = (
        jnp.einsum("tunk,tunl->tukl", update, update, preferred_element_type=jnp.float32)
        / row_count
    ).astype(jnp.bfloat16)
    return (update, gram)


def solution(mesh):
    in_specs = (P("row", "col", None), P("row", "col", None), P("col", None), P())
    out_specs = (P("row", "col", None, None), P("row", "col", None, None))
    return jax.shard_map(local, mesh=mesh, in_specs=in_specs, out_specs=out_specs, check_vma=False)
```

profile of v0, /device:TPU:1, one launch (start us, length us, event | category | flops | bytes accessed | tf_op | source)
XLA Modules:
  0.0 429.4 jit_solution(2731920971503622483)
XLA Ops:
  7.2 0.0 all-gather.4.cloned.1.call-start
  7.2 2.1 copy.6
  9.3 0.0 all-gather.4.cloned.1.call-update
  9.3 0.0 all-gather.8.cloned.1.call-start
  9.4 2.1 copy.7
  11.5 0.0 all-gather.8.cloned.1.call-update
  11.5 0.0 all-gather.6.cloned.1.call-start
  11.5 78.4 %all-gather.4.cloned.1.call-done = bf16[4,2048,512]{1,2,0:T(8,128)(2,1)} async-done(((bf16[4,128,512]{1,2,0:T(8,128)(2,1)}), bf16[4,2048,512]{1,2,0:T(8,128)(2,1)}) %all-gather.4.cloned.1.call-update) | async-done | bytes 8388624 | tf_op jit(solution)/shard_map/all_gather | solution.py:20
  89.9 6.5 %fusion.13 = bf16[4,128,512]{1,2,0:T(8,128)(2,1)} fusion(bf16[4,2048,512]{1,2,0:T(8,128)(2,1)} %all-gather.4.cloned.1.call-done, bf16[128,2048]{1,0:T(8,128)(2,1)S(1)} %copy-done), kind=kOutput, calls=%fused_computation.13 | convolution fusion | flops 1074003968 | bytes 9437184 | tf_op jit(solution)/shard_map/rn,tnk->trk/dot_general | solution.py:21
  96.4 0.0 all-gather.6.cloned.1.call-update
  96.5 0.0 all-reduce.3.cloned.1.call-start
  96.5 72.1 %all-gather.8.cloned.1.call-done = bf16[4,2048,512]{1,2,0:T(8,128)(2,1)} async-done(((bf16[4,128,512]{1,2,0:T(8,128)(2,1)}), bf16[4,2048,512]{1,2,0:T(8,128)(2,1)}) %all-gather.8.cloned.1.call-update) | async-done | bytes 8388624 | tf_op jit(solution)/shard_map/all_gather | solution.py:26
  168.7 4.5 %dynamic-slice_select_fusion = bf16[2,2048,512]{1,2,0:T(8,128)(2,1)} fusion(bf16[4,2048,512]{1,2,0:T(8,128)(2,1)} %all-gather.8.cloned.1.call-done, s32[]{:T(128)S(6)} %select_n.36, pred[]{:T(512)S(6)} %eq.6), kind=kLoop, calls=%fused_computation.8 | loop fusion | flops 2097152 | bytes 8388613 | tf_op jit(solution)/shard_map/jit(_where)/select_n | solution.py:9
  173.1 74.9 %all-gather.6.cloned.1.call-done = bf16[4,2048,512]{1,2,0:T(8,128)(2,1)} async-done(((bf16[4,128,512]{1,2,0:T(8,128)(2,1)}), bf16[4,2048,512]{1,2,0:T(8,128)(2,1)}) %all-gather.6.cloned.1.call-update) | async-done | bytes 8388624 | tf_op jit(solution)/shard_map/all_gather | solution.py:25
  248.0 4.5 %dynamic-slice_select_fusion.1 = bf16[2,2048,512]{1,2,0:T(8,128)(2,1)} fusion(bf16[4,2048,512]{1,2,0:T(8,128)(2,1)} %all-gather.6.cloned.1.call-done, s32[]{:T(128)S(6)} %select_n.36, pred[]{:T(512)S(6)} %eq.6), kind=kLoop, calls=%fused_computation.11 | loop fusion | flops 2097152 | bytes 8388613 | tf_op jit(solution)/shard_map/jit(_where)/select_n | solution.py:9
  252.5 0.0 all-reduce.3.cloned.1.call-update
  252.5 0.1 dynamic_slice.14
  252.6 0.1 dynamic_slice.13
  252.7 0.1 compare_convert_fusion
  252.7 0.1 fusion.15
  252.8 104.1 %all-reduce.3.cloned.1.call-done = (bf16[2,2048,512]{1,2,0:T(8,128)(2,1)}, bf16[2,2048,512]{1,2,0:T(8,128)(2,1)}) async-done(((bf16[2,2048,512]{1,2,0:T(8,128)(2,1)}, bf16[2,2048,512]{1,2,0:T(8,128)(2,1)}), (bf16[2,2048,512]{1,2,0:T(8,128)(2,1)}, bf16[2,2048,512]{1,2,0:T(8,128)(2,1)})) %all-reduce.3.cloned.1.call-update) | async-done | bytes 8388624 | tf_op jit(solution)/shard_map/psum | solution.py:9
  356.9 25.6 %convert_bitcast_fusion = bf16[4,2,2048,512]{2,3,0,1:T(8,128)(2,1)} fusion(bf16[4,2048,512]{1,2,0:T(8,128)(2,1)} %all-gather.6.cloned.1.call-done, bf16[2,2048,512]{1,2,0:T(8,128)(2,1)} %get-tuple-element.4, bf16[2,2048,512]{1,2,0:T(8,128)(2,1)} %get-tuple-element.5, f32[2,512]{1,0:T(2,128)S(1)} %compare_convert_fusion, f32[4,512]{1,0:T(4,128)S(1)} %fusion.15), kind=kOutput, calls=%fused_computation | convolution fusion | flops 17194549248 | bytes 33566720 | tf_op jit(solution)/shard_map/unl,tukl->tunk/dot_general | solution.py:44
  382.6 21.6 %copy.11 = bf16[4,2,2048,512]{3,2,1,0:T(8,128)(2,1)} copy(bf16[4,2,2048,512]{2,3,0,1:T(8,128)(2,1)} %convert_bitcast_fusion) | data formatting | bytes 33554432 | tf_op jit(solution)/shard_map/convert_element_type | solution.py:46
  404.2 18.7 %multiply_convert_fusion = bf16[4,2,512,512]{3,2,1,0:T(8,128)(2,1)} fusion(bf16[4,2,2048,512]{3,2,1,0:T(8,128)(2,1)} %copy.11), kind=kOutput, calls=%fused_computation.3 | convolution fusion | flops 8594128896 | bytes 20971520 | tf_op jit(solution)/shard_map/tunk,tunl->tukl/dot_general | solution.py:48
  (6 shorter events, 0.0 us)
Async XLA Ops:
  7.2 82.7 %copy-start = (bf16[128,2048]{1,0:T(8,128)(2,1)S(1)}, bf16[128,2048]{1,0:T(8,128)(2,1)}, u32[]{:S(2)}) copy-start(bf16[128,2048]{1,0:T(8,128)(2,1)} %param.6) | copy-start | bytes 1572868
  7.2 82.7 %all-gather.4.cloned.1.call-start = ((), (), s32[]{:S(2)}) async-start(), calls=%async_computation | async-start | bytes 8912896 | tf_op jit(solution)/shard_map/all_gather | solution.py:20
  9.3 159.3 %all-gather.8.cloned.1.call-start = ((), (), s32[]{:S(2)}) async-start(), calls=%async_computation.2 | async-start | bytes 8912896 | tf_op jit(solution)/shard_map/all_gather | solution.py:26
  11.5 236.5 %all-gather.6.cloned.1.call-start = ((), (), s32[]{:S(2)}) async-start(), calls=%async_computation.1 | async-start | bytes 8912896 | tf_op jit(solution)/shard_map/all_gather | solution.py:25
  96.5 260.5 %all-reduce.3.cloned.1.call-start = ((), (), s32[]{:S(2)}) async-start(), calls=%async_computation.3 | async-start | bytes 16777216 | tf_op jit(solution)/shard_map/psum | solution.py:9
  173.1 79.4 %copy-start.2 = (s32[32]{0:T(128)S(1)}, s32[32]{0:T(128)}, u32[]{:S(2)}) copy-start(s32[32]{0:T(128)} %param.7) | copy-start | bytes 388
  404.2 18.7 %copy-start.1 = (bf16[128,2048]{1,0:T(8,128)(2,1)S(1)}, bf16[128,2048]{1,0:T(8,128)(2,1)}, u32[]{:S(2)}) copy-start(bf16[128,2048]{1,0:T(8,128)(2,1)} %param.6) | copy-start | bytes 1572868
Sparse Core Ops, SparseCore 0:
  10.7 79.1 all-gather.3
  92.0 76.6 all-gather.7
  171.3 76.6 all-gather.5
  252.6 104.2 all-reduce.2
where the time goes:
time: 430 us; the launch traced here: 429 us
  waiting for transfers between devices  330 us (77%)
  matrix products  50.8 us (12%)
  local copies, waits for them, and re-layouts  25.9 us (6%)
  between operations  13.8 us (3%)
  other arithmetic  9.09 us (2%)
    psum x1, waiting for transfers between devices, from_root(): return lax.psum(jnp.where(mine, array, jnp.zeros_like(array)), axis)  104 us
    all_gather x1, waiting for transfers between devices, local(): full_right = lax.all_gather(pan_right, 'col', axis=1, tiled=True)  78.4 us
    all_gather x1, waiting for transfers between devices, local(): lax.all_gather(solved_slab, 'col', axis=1, tiled=True)  74.9 us
    all_gather x1, waiting for transfers between devices, local(): lax.all_gather(pan_left, 'col', axis=1, tiled=True)  72.1 us
    dot_general x1, matrix products, local(): jnp.einsum('unl,tukl->tunk', col_left, core, preferred_element_type=jnp.f...  25.6 us
    convert_element_type x1, local copies, waits for them, and re-layouts, local(): update = jnp.einsum('unl,tukl->tunk', col_left, core, preferred_element_t...  21.6 us
    dot_general x1, matrix products, local(): jnp.einsum('tunk,tunl->tukl', update, update, preferred_element_type=jnp....  18.7 us
    select_n x2, other arithmetic, from_root(): return lax.psum(jnp.where(mine, array, jnp.zeros_like(array)), axis)  8.95 us
  transfers between devices with their start and end apart: 4, of which 4 were waited for; matrix products, arithmetic and copies ran while one was open for 3% of the time, Pallas kernels for 0%

commit v1 on v0

v1 whole, which is shorter than its diff:
```python
import functools

import jax
import jax.numpy as jnp
from jax import lax
from jax.experimental import pallas as pl
from jax.experimental.pallas import tpu as pltpu
from jax.sharding import PartitionSpec as P

MESH = pl.DeviceIdType.MESH
BF = jnp.bfloat16
F32 = jnp.float32


def device(x, y, z, p):
    return (lax.rem(y, 4) * 2 + p, lax.rem(z, 4) * 4 + lax.rem(x, 4))


def run_if(condition, body):
    if condition is None:
        body()
    else:
        pl.when(condition)(body)


class Semaphores:
    def __init__(self, send, recv):
        self.send, self.recv, self.used = send, recv, 0

    def take(self, count):
        first = self.used
        self.used += count
        return first

    def copy(self, src, dst, send, recv, target):
        return pltpu.make_async_remote_copy(
            src_ref=src, dst_ref=dst, send_sem=self.send.at[send], recv_sem=self.recv.at[recv],
            device_id=target, device_id_type=MESH,
        )


class Ring:
    def __init__(self, sems, me, plus, minus, view, half, has=lambda slot: None):
        self.sems, self.plus, self.minus = sems, plus, minus
        self.view, self.half, self.has = view, half, has
        self.me, self.left, self.right, self.far = me, lax.rem(me + 3, 4), lax.rem(me + 1, 4), lax.rem(me + 2, 4)
        self.base = sems.take(4)

    def message(self, ref, which, target):
        return self.sems.copy(ref, ref, self.base + which, self.base + which, target)

    def start(self):
        def go():
            self.message(self.view(self.me), 0, self.plus).start()
            self.message(self.view(self.me), 1, self.minus).start()

        run_if(self.has(self.me), go)

    def forward(self):
        def from_left():
            self.message(self.view(self.left), 0, self.plus).wait_recv()
            self.message(self.half(self.left, 0), 2, self.plus).start()

        def from_right():
            self.message(self.view(self.right), 1, self.minus).wait_recv()
            self.message(self.half(self.right, 1), 3, self.minus).start()

        run_if(self.has(self.left), from_left)
        run_if(self.has(self.right), from_right)

    def finish(self):
        def go():
            self.message(self.half(self.far, 0), 2, self.plus).wait_recv()
            self.message(self.half(self.far, 1), 3, self.minus).wait_recv()

        run_if(self.has(self.far), go)

    def drain(self):
        def own():
            self.message(self.view(self.me), 0, self.plus).wait_send()
            self.message(self.view(self.me), 1, self.minus).wait_send()

        run_if(self.has(self.me), own)
        run_if(self.has(self.left), lambda: self.message(self.half(self.left, 0), 2, self.plus).wait_send())
        run_if(self.has(self.right), lambda: self.message(self.half(self.right, 1), 3, self.minus).wait_send())


def dot_tn(a, b):
    return lax.dot_general(a, b, (((0,), (0,)), ((), ())), preferred_element_type=F32)


def gather_kernel(
    left_ref, right_ref, inv_ref, rank_ref, core_out, left_out,
    rbuf, abuf, wbuf, lbuf, rjp, sjp, cores, send_sem, recv_sem, local_sem,
):
    row, col = lax.axis_index("row"), lax.axis_index("col")
    x, z, y, p = lax.rem(col, 4), lax.div(col, 4), lax.div(row, 2), lax.rem(row, 2)
    xp, xm = device(x + 1, y, z, p), device(x + 3, y, z, p)
    yp, ym = device(x, y + 1, z, p), device(x, y + 3, z, p)
    zp, zm = device(x, y, z + 1, p), device(x, y, z + 3, p)
    mate = device(x, y, z, 1 - p)
    sems = Semaphores(send_sem, recv_sem)

    own_right = pltpu.make_async_copy(right_ref, rbuf.at[:, z, x], local_sem.at[0])
    own_right.start()
    own_inv = [pltpu.make_async_copy(inv_ref.at[p, :, :, 512 * k:512 * k + 512], abuf.at[k, z, x, p], local_sem.at[1 + k]) for k in range(4)]
    for k in range(4):
        own_inv[k].start()

    barrier = pltpu.get_barrier_semaphore()
    for target in (xp, xm, yp, ym, zp, zm, mate):
        pl.semaphore_signal(barrier, inc=1, device_id=target, device_id_type=MESH)
    for source in range(16):
        pl.semaphore_signal(barrier, inc=1, device_id=device(source % 4, z, source // 4, lax.div(x, 2)), device_id_type=MESH)
    pl.semaphore_wait(barrier, 23)

    pieces = sems.take(32)
    at_home = jnp.logical_and(y == z, p == lax.div(x, 2))

    def piece(which, m):
        edge, y_to, p_to = m // 8, (m // 2) % 4, m % 2
        x_to = 2 * p + edge
        columns = slice(128 * y_to, 128 * y_to + 128)
        mine = jnp.logical_and(jnp.logical_and(at_home, x_to == x), jnp.logical_and(y_to == y, p_to == p))
        if which == 0:
            src, dst = right_ref.at[2 * edge + p_to, :, :, columns], rjp.at[col]
        else:
            src, dst = left_ref.at[2 * edge + p_to, :, :, columns], lbuf.at[p_to, col, :, :, columns]
        remote = sems.copy(src, dst, pieces + 16 * which + m, pieces + 16 * which + col, device(x_to, y_to, y, p_to))
        return mine, pltpu.make_async_copy(src, dst, local_sem.at[5 + which]), remote

    def send_pieces(which):
        for m in range(16):
            mine, local, remote = piece(which, m)
            pl.when(mine)(local.start)
            pl.when(jnp.logical_not(mine))(remote.start)

    def take_pieces(which):
        ycol = pl.ds(pl.multiple_of(128 * y, 128), 128)
        for source in range(16):
            dst = rjp.at[source] if which == 0 else lbuf.at[p, source, :, :, ycol]
            mine = jnp.logical_and(at_home, col == source)
            pl.when(mine)(pltpu.make_async_copy(dst, dst, local_sem.at[5 + which]).wait)
            pl.when(jnp.logical_not(mine))(sems.copy(dst, dst, pieces + 16 * which, pieces + 16 * which + source, mate).wait_recv)

    def drain_pieces(which):
        for m in range(16):
            mine, _, remote = piece(which, m)
            pl.when(jnp.logical_not(mine))(remote.wait_send)

    def right_rings(t):
        return (
            Ring(sems, x, xp, xm, lambda s: rbuf.at[t, z, s, 0], lambda s, h: rbuf.at[t, z, s, 0, pl.ds(32 * h, 32)]),
            Ring(sems, z, zp, zm, lambda s: rbuf.at[t, s, x, 1], lambda s, h: rbuf.at[t, s, x, 1, pl.ds(32 * h, 32)]),
            Ring(sems, z, zp, zm, lambda s: rbuf.at[t, s, :, 0], lambda s, h: rbuf.at[t, s, pl.ds(2 * h, 2), 0]),
            Ring(sems, x, xp, xm, lambda s: rbuf.at[t, :, s, 1], lambda s, h: rbuf.at[t, pl.ds(2 * h, 2), s, 1]),
        )

    def inv_rings(k):
        return (
            Ring(sems, x, xp, xm, lambda s: abuf.at[k, z, s, p, 0], lambda s, h: abuf.at[k, z, s, p, 0, pl.ds(16 * h, 16)],
                 lambda s: None if k == 0 else z >= k),
            Ring(sems, z, zp, zm, lambda s: abuf.at[k, s, x, p, 1], lambda s, h: abuf.at[k, s, x, p, 1, pl.ds(16 * h, 16)],
                 lambda s: None if k == 0 else s >= k),
            Ring(sems, z, zp, zm, lambda s: abuf.at[k, s, :, p, 0], lambda s, h: abuf.at[k, s, pl.ds(2 * h, 2), p, 0],
                 lambda s: None if k == 0 else s >= k),
            Ring(sems, x, xp, xm, lambda s: abuf.at[k, pl.ds(k, 4 - k), s, p, 1],
                 lambda s, h: abuf.at[k, pl.ds(k, 4 - k), s, p, 1, pl.ds(16 * h, 16)]),
        )

    right = [right_rings(t) for t in range(4)]
    inv = [inv_rings(k) for k in range(4)]

    def first_start(group):
        for rings in group:
            rings[0].start()
            rings[1].start()

    def first_forward(group):
        for rings in group:
            rings[0].forward()
            rings[1].forward()

    def second_start(group):
        for rings in group:
            rings[0].finish()
            rings[2].start()
            rings[1].finish()
            rings[3].start()

    def second_forward(group):
        for rings in group:
            rings[2].forward()
            rings[3].forward()

    def second_finish(group):
        for rings in group:
            rings[2].finish()
            rings[3].finish()

    def column_chunk(s):
        return pl.ds(pl.multiple_of(128 * s, 128), 128)

    l_ring = Ring(sems, y, yp, ym, lambda s: lbuf.at[p, :, :, :, column_chunk(s)], lambda s, h: lbuf.at[p, pl.ds(8 * h, 8), :, :, column_chunk(s)])
    w_ring = Ring(sems, y, yp, ym, lambda s: wbuf.at[p, :, column_chunk(s)], lambda s, h: wbuf.at[p, pl.ds(1024 * h, 1024), column_chunk(s)])
    swaps = {"l": sems.take(4), "w": sems.take(4), "a": sems.take(4)}

    def swap(kind, slot, ref):
        return sems.copy(ref, ref, swaps[kind] + slot, swaps[kind] + slot, mate)

    def other(ring, kind, n, owner):
        s = (ring.me, ring.left, ring.right, ring.far)[n]
        buf = lbuf if kind == "l" else wbuf
        ref = buf.at[owner, :, :, :, column_chunk(s)] if kind == "l" else buf.at[owner, :, column_chunk(s)]
        return swap(kind, n, ref)

    def inv_half(k, owner):
        return abuf.at[k, pl.ds(k, 4 - k), :, owner]

    def compute_w():
        for b in range(4):
            acc = None
            for k in range(b + 1):
                term = jnp.dot(abuf[k, b].reshape(512, 512), rjp[4 * k:4 * k + 4].reshape(512, 128), preferred_element_type=F32)
                acc = term if acc is None else acc + term
            sjp[b] = acc.astype(BF)
        for k in range(4):
            acc = None
            for b in range(k, 4):
                term = dot_tn(abuf[k, b].reshape(512, 512), sjp[b])
                acc = term if acc is None else acc + term
            wbuf[p, 512 * k:512 * k + 512, column_chunk(y)] = acc.astype(BF)

    def core_copy(j, t):
        return pltpu.make_async_copy(cores.at[j, t], core_out.at[j, t], local_sem.at[7 + 2 * t + j])

    def compute_core(t):
        rank_i = rank_ref[4 * row + t]
        k_live = lax.broadcasted_iota(jnp.int32, (512, 512), 1) < rank_i

        @pl.loop(0, 2)
        def _(j):
            rank_j = rank_ref[2 * col + j]
            l_live = lax.broadcasted_iota(jnp.int32, (512, 512), 0) < rank_j
            acc = dot_tn(wbuf[j], rbuf[t].reshape(2048, 512))
            cores[j, t] = jnp.where(jnp.logical_and(k_live, l_live), acc, 0.0).astype(BF)

        for j in range(2):
            core_copy(j, t).start()

    left_copy = pltpu.make_async_copy(lbuf, left_out, local_sem.at[15])

    for k in range(4):
        own_inv[k].wait()
    own_right.wait()
    send_pieces(0)
    first_start(inv)
    send_pieces(1)
    first_start(right[:1])
    first_forward(inv)
    second_start(inv)
    first_forward(right[:1])
    first_start(right[1:2])
    take_pieces(1)
    l_ring.start()
    other(l_ring, "l", 0, p).start()
    second_forward(inv)
    second_start(right[:1])
    first_forward(right[1:2])
    first_start(right[2:3])
    second_finish(inv)
    for k in range(4):
        swap("a", k, inv_half(k, p)).start()
    take_pieces(0)
    l_ring.forward()
    for k in range(4):
        swap("a", k, inv_half(k, 1 - p)).wait_recv()
    second_forward(right[:1])
    second_start(right[1:2])
    first_forward(right[2:3])
    first_start(right[3:4])
    compute_w()
    w_ring.start()
    other(w_ring, "w", 0, p).start()
    l_ring.finish()
    for n in range(1, 4):
        other(l_ring, "l", n, p).start()
    second_finish(right[:1])
    second_forward(right[1:2])
    second_start(right[2:3])
    first_forward(right[3:4])
    w_ring.forward()
    second_finish(right[1:2])
    second_forward(right[2:3])
    second_start(right[3:4])
    w_ring.finish()
    for n in range(1, 4):
        other(w_ring, "w", n, p).start()
    for n in range(4):
        other(l_ring, "l", n, 1 - p).wait_recv()
    left_copy.start()
    for n in range(4):
        other(w_ring, "w", n, 1 - p).wait_recv()
    compute_core(0)
    second_finish(right[2:3])
    second_forward(right[3:4])
    compute_core(1)
    compute_core(2)
    second_finish(right[3:4])
    compute_core(3)

    for which in range(2):
        drain_pieces(which)
    for rings in inv + right:
        for ring in rings:
            ring.drain()
    l_ring.drain()
    w_ring.drain()
    for n in range(4):
        other(l_ring, "l", n, p).wait_send()
        other(w_ring, "w", n, p).wait_send()
        swap("a", n, inv_half(n, p)).wait_send()
    left_copy.wait()
    for t in range(4):
        for j in range(2):
            core_copy(j, t).wait()


def gather(pan_left, pan_right, inverse, rank_list):
    return pl.pallas_call(
        gather_kernel,
        out_shape=(jax.ShapeDtypeStruct((2, 4, 512, 512), BF), jax.ShapeDtypeStruct((2, 16, 2, 64, 512), BF)),
        in_specs=[pl.BlockSpec(memory_space=pltpu.VMEM)] * 3 + [pl.BlockSpec(memory_space=pltpu.SMEM)],
        out_specs=(pl.BlockSpec(memory_space=pl.ANY), pl.BlockSpec(memory_space=pl.ANY)),
        scratch_shapes=[
            pltpu.VMEM((4, 4, 4, 2, 64, 512), BF),
            pltpu.VMEM((4, 4, 4, 2, 2, 32, 512), BF),
            pltpu.VMEM((2, 2048, 512), BF),
            pltpu.VMEM((2, 16, 2, 64, 512), BF),
            pltpu.VMEM((16, 2, 64, 128), BF),
            pltpu.VMEM((4, 512, 128), BF),
            pltpu.VMEM((2, 4, 512, 512), BF),
            pltpu.SemaphoreType.DMA((192,)),
            pltpu.SemaphoreType.DMA((192,)),
            pltpu.SemaphoreType.DMA((16,)),
        ],
        compiler_params=pltpu.CompilerParams(collective_id=0, has_side_effects=True, vmem_limit_bytes=60 << 20),
        name="gather",
    )(pan_left.reshape(4, 2, 64, 512), pan_right.reshape(4, 2, 64, 512), inverse.reshape(2, 2, 32, 2048), rank_list)


def update_kernel(core_ref, left_ref, update_ref, gram_ref):
    update = jnp.dot(left_ref[0], core_ref[0, 0], preferred_element_type=F32).astype(BF)
    update_ref[0, 0] = update
    gram_ref[0, 0] = (dot_tn(update_ref[0, 0], update_ref[0, 0]) * (1.0 / 2048)).astype(BF)


def local(pan_left, pan_right, inverse, rank_list):
    core, left = gather(pan_left, pan_right, inverse, rank_list)
    return pl.pallas_call(
        update_kernel,
        grid=(2, 4),
        out_shape=(jax.ShapeDtypeStruct((4, 2, 2048, 512), BF), jax.ShapeDtypeStruct((4, 2, 512, 512), BF)),
        in_specs=[
            pl.BlockSpec((1, 1, 512, 512), lambda j, i: (j, i, 0, 0)),
            pl.BlockSpec((1, 2048, 512), lambda j, i: (j, 0, 0)),
        ],
        out_specs=(
            pl.BlockSpec((1, 1, 2048, 512), lambda j, i: (i, j, 0, 0)),
            pl.BlockSpec((1, 1, 512, 512), lambda j, i: (i, j, 0, 0)),
        ),
        compiler_params=pltpu.CompilerParams(vmem_limit_bytes=48 << 20),
        name="update",
    )(core, left.reshape(2, 2048, 512))


def solution(mesh):
    in_specs = (P("row", "col", None), P("row", "col", None), P("col", None), P())
    out_specs = (P("row", "col", None, None), P("row", "col", None, None))
    return jax.shard_map(local, mesh=mesh, in_specs=in_specs, out_specs=out_specs, check_vma=False)
```

time: 430 us -> 122 us (0.28)
  waiting for transfers between devices: 330 us -> 0 us
  Pallas kernels: 0 us -> 119 us
  matrix products: 50.8 us -> 0 us
  local copies, waits for them, and re-layouts: 25.9 us -> 2.18 us
  between operations: 13.8 us -> 0.65 us
  other arithmetic: 9.09 us -> 0 us
    all_gather x3 -> x0, waiting for transfers between devices: 225 us -> none  [the longest x1 78.4 us: local(): full_right = lax.all_gather(pan_right, 'col', axis=1, tiled=True)]
    pallas_call x0 -> x2, Pallas kernels: none -> 119 us  [the longest x1 97.4 us: gather(): pl.pallas_call(gather_kernel, out_shape=(jax.ShapeDtypeStruct((2, 4, 512,...]
    psum x1 -> x0, waiting for transfers between devices: 104 us -> none  [from_root(): return lax.psum(jnp.where(mine, array, jnp.zeros_like(array)), axis)]
    dot_general x3 -> x0, matrix products: 50.8 us -> none  [the longest x1 25.6 us: local(): jnp.einsum('unl,tukl->tunk', col_left, core, preferred_element_type=jnp.f...]
    convert_element_type x1 -> x0, local copies, waits for them, and re-layouts: 21.6 us -> none  [local(): update = jnp.einsum('unl,tukl->tunk', col_left, core, preferred_element_t...]
    select_n x2 -> x0, other arithmetic: 8.95 us -> none  [from_root(): return lax.psum(jnp.where(mine, array, jnp.zeros_like(array)), axis)]
  transfers between devices with their start and end apart: 4 -> 0, of which waited for: 4 -> 0; matrix products, arithmetic and copies ran while one was open for 3% -> 0% of each run, Pallas kernels for 0% -> 0%
where the time goes in v1:
time: 122 us
  Pallas kernels  119 us (98%)
  local copies, waits for them, and re-layouts  2.18 us (2%)
    pallas_call x1, Pallas kernels, gather(): pl.pallas_call(gather_kernel, out_shape=(jax.ShapeDtypeStruct((2, 4, 512,...  97.4 us
    pallas_call x1, Pallas kernels, local(): pl.pallas_call(update_kernel, grid=(2, 4), out_shape=(jax.ShapeDtypeStruc...  21.3 us

profile of v1, /device:TPU:1, one launch (start us, length us, event | category | flops | bytes accessed | tf_op | source)
XLA Modules:
  0.0 121.5 jit_solution(13910971423386725930)
XLA Ops:
  0.6 97.4 %gather.1 = (bf16[2,4,512,512]{3,2,1,0:T(8,128)(2,1)}, bf16[2,16,2,64,512]{4,3,2,1,0:T(8,128)(2,1)}) custom-call(bf16[4,2,64,512]{3,2,1,0:T(8,128)(2,1)} %bitcast.5, bf16[4,2,64,512]{3,2,1,0:T(8,128)(2,1)} %bitcast.6, bf16[2,2,32,2048]{3,2,1,0:T(8,128)(2,1)} %bitcast.7, s32[32]{0:T(128)} %rank_ref.1), custom_call_target="tpu_custom_call" | custom-call | tf_op jit(solution)/shard_map/gather/pallas_call | solution.py:330
  98.1 0.0 copy-start
  98.1 2.2 %copy-done = bf16[2,4,512,512]{3,2,1,0:T(8,128)(2,1)S(1)} copy-done((bf16[2,4,512,512]{3,2,1,0:T(8,128)(2,1)S(1)}, bf16[2,4,512,512]{3,2,1,0:T(8,128)(2,1)}, u32[]{:S(2)}) %copy-start) | copy-done | bytes 4194328
  100.3 21.3 %update.1 = (bf16[4,2,2048,512]{3,2,1,0:T(8,128)(2,1)}, bf16[4,2,512,512]{3,2,1,0:T(8,128)(2,1)}) custom-call(bf16[2,4,512,512]{3,2,1,0:T(8,128)(2,1)S(1)} %copy-done, bf16[2,2048,512]{2,1,0:T(8,128)(2,1)} %bitcast.4), custom_call_target="tpu_custom_call" | custom-call | tf_op jit(solution)/shard_map/update/pallas_call | solution.py:360
Async XLA Ops:
  98.1 2.2 %copy-start = (bf16[2,4,512,512]{3,2,1,0:T(8,128)(2,1)S(1)}, bf16[2,4,512,512]{3,2,1,0:T(8,128)(2,1)}, u32[]{:S(2)}) copy-start(bf16[2,4,512,512]{3,2,1,0:T(8,128)(2,1)} %get-tuple-element.4.core_ref) | copy-start | bytes 12582916

commit v2 on v1

v2 whole, which is shorter than its diff:
```python
import functools

import jax
import jax.numpy as jnp
from jax import lax
from jax.experimental import pallas as pl
from jax.experimental.pallas import tpu as pltpu
from jax.sharding import PartitionSpec as P

MESH = pl.DeviceIdType.MESH
BF = jnp.bfloat16
F32 = jnp.float32
SPLIT = 80


def device(x, y, z, p):
    return (lax.rem(y, 4) * 2 + p, lax.rem(z, 4) * 4 + lax.rem(x, 4))


def run_if(condition, body):
    if condition is None:
        body()
    else:
        pl.when(condition)(body)


class Semaphores:
    def __init__(self, send, recv):
        self.send, self.recv, self.used = send, recv, 0

    def take(self, count):
        first = self.used
        self.used += count
        return first

    def copy(self, src, dst, send, recv, target):
        return pltpu.make_async_remote_copy(
            src_ref=src, dst_ref=dst, send_sem=self.send.at[send], recv_sem=self.recv.at[recv],
            device_id=target, device_id_type=MESH,
        )


class Ring:
    def __init__(self, sems, me, plus, minus, view, half, has=lambda slot: None):
        self.sems, self.plus, self.minus = sems, plus, minus
        self.view, self.half, self.has = view, half, has
        self.me, self.left, self.right, self.far = me, lax.rem(me + 3, 4), lax.rem(me + 1, 4), lax.rem(me + 2, 4)
        self.base = sems.take(4)

    def message(self, ref, which, target):
        return self.sems.copy(ref, ref, self.base + which, self.base + which, target)

    def start(self):
        def go():
            self.message(self.view(self.me), 0, self.plus).start()
            self.message(self.view(self.me), 1, self.minus).start()

        run_if(self.has(self.me), go)

    def forward(self):
        def from_left():
            self.message(self.view(self.left), 0, self.plus).wait_recv()
            self.message(self.half(self.left, 0), 2, self.plus).start()

        def from_right():
            self.message(self.view(self.right), 1, self.minus).wait_recv()
            self.message(self.half(self.right, 1), 3, self.minus).start()

        run_if(self.has(self.left), from_left)
        run_if(self.has(self.right), from_right)

    def finish(self):
        def go():
            self.message(self.half(self.far, 0), 2, self.plus).wait_recv()
            self.message(self.half(self.far, 1), 3, self.minus).wait_recv()

        run_if(self.has(self.far), go)

    def drain(self):
        def own():
            self.message(self.view(self.me), 0, self.plus).wait_send()
            self.message(self.view(self.me), 1, self.minus).wait_send()

        run_if(self.has(self.me), own)
        run_if(self.has(self.left), lambda: self.message(self.half(self.left, 0), 2, self.plus).wait_send())
        run_if(self.has(self.right), lambda: self.message(self.half(self.right, 1), 3, self.minus).wait_send())


def dot_tn(a, b):
    return lax.dot_general(a, b, (((0,), (0,)), ((), ())), preferred_element_type=F32)


def gather_kernel(
    left_ref, right_ref, inv_ref, rank_ref, cores, left_out, grams,
    rbuf, abuf, wbuf, lbuf, rj, sj, weight, send_sem, recv_sem, local_sem,
):
    row, col = lax.axis_index("row"), lax.axis_index("col")
    x, z, y, p = lax.rem(col, 4), lax.div(col, 4), lax.div(row, 2), lax.rem(row, 2)
    xp, xm = device(x + 1, y, z, p), device(x + 3, y, z, p)
    yp, ym = device(x, y + 1, z, p), device(x, y + 3, z, p)
    zp, zm = device(x, y, z + 1, p), device(x, y, z + 3, p)
    mate = device(x, y, z, 1 - p)
    sems = Semaphores(send_sem, recv_sem)

    own_right = pltpu.make_async_copy(right_ref, rbuf.at[:, z, x], local_sem.at[0])
    own_right.start()
    own_inv = [pltpu.make_async_copy(inv_ref.at[p, :, 512 * k:512 * k + 512], abuf.at[k, z, x, p], local_sem.at[1 + k]) for k in range(4)]
    for k in range(4):
        own_inv[k].start()

    barrier = pltpu.get_barrier_semaphore()
    for target in (xp, xm, yp, ym, zp, zm, mate):
        pl.semaphore_signal(barrier, inc=1, device_id=target, device_id_type=MESH)
    for source in range(16):
        pl.semaphore_signal(barrier, inc=1, device_id=device(source % 4, z, source // 4, lax.div(x, 2)), device_id_type=MESH)
    pl.semaphore_wait(barrier, 23)

    pieces = sems.take(32)
    at_home = jnp.logical_and(y == z, p == lax.div(x, 2))

    def piece(which, m):
        edge, y_to, p_to = m // 8, (m // 2) % 4, m % 2
        x_to = 2 * p + edge
        columns = slice(128 * y_to, 128 * y_to + 128)
        mine = jnp.logical_and(jnp.logical_and(at_home, x_to == x), jnp.logical_and(y_to == y, p_to == p))
        if which == 0:
            src, dst = rbuf.at[2 * edge + p_to, z, x, :, columns], rj.at[col, :, columns]
        else:
            src, dst = left_ref.at[2 * edge + p_to, :, columns], lbuf.at[p_to, col, :, columns]
        remote = sems.copy(src, dst, pieces + 16 * which + m, pieces + 16 * which + col, device(x_to, y_to, y, p_to))
        return mine, pltpu.make_async_copy(src, dst, local_sem.at[5 + which]), remote

    def send_pieces(which):
        for m in range(16):
            mine, local, remote = piece(which, m)
            pl.when(mine)(local.start)
            pl.when(jnp.logical_not(mine))(remote.start)

    def take_pieces(which):
        ycol = pl.ds(pl.multiple_of(128 * y, 128), 128)
        for source in range(16):
            dst = rj.at[source, :, ycol] if which == 0 else lbuf.at[p, source, :, ycol]
            mine = jnp.logical_and(at_home, col == source)
            pl.when(mine)(pltpu.make_async_copy(dst, dst, local_sem.at[5 + which]).wait)
            pl.when(jnp.logical_not(mine))(sems.copy(dst, dst, pieces + 16 * which, pieces + 16 * which + source, mate).wait_recv)

    def drain_pieces(which):
        for m in range(16):
            mine, _, remote = piece(which, m)
            pl.when(jnp.logical_not(mine))(remote.wait_send)

    first, second = pl.ds(0, SPLIT), pl.ds(SPLIT, 128 - SPLIT)

    def side(h):
        return pl.ds(256 * h, 256)

    def right_rings(t):
        return (
            Ring(sems, x, xp, xm, lambda s: rbuf.at[t, z, s, first], lambda s, h: rbuf.at[t, z, s, first, side(h)]),
            Ring(sems, z, zp, zm, lambda s: rbuf.at[t, s, x, second], lambda s, h: rbuf.at[t, s, x, second, side(h)]),
            Ring(sems, z, zp, zm, lambda s: rbuf.at[t, s, :, first], lambda s, h: rbuf.at[t, s, pl.ds(2 * h, 2), first]),
            Ring(sems, x, xp, xm, lambda s: rbuf.at[t, :, s, second], lambda s, h: rbuf.at[t, pl.ds(2 * h, 2), s, second]),
        )

    def inv_rings(k):
        return (
            Ring(sems, z, zp, zm, lambda s: abuf.at[k, s, x, p], lambda s, h: abuf.at[k, s, x, p, pl.ds(32 * h, 32)],
                 lambda s: None if k == 0 else s >= k),
            Ring(sems, x, xp, xm, lambda s: abuf.at[k, pl.ds(k, 4 - k), s, p],
                 lambda s, h: abuf.at[k, pl.ds(k, 4 - k), s, p, pl.ds(32 * h, 32)]),
        )

    right = [right_rings(t) for t in range(4)]
    inv = [inv_rings(k) for k in range(4)]

    def start(stage, tiles):
        for t in tiles:
            right[t][stage].start()

    def forward(stage, tiles):
        for t in tiles:
            right[t][stage].forward()

    def finish(stage, tiles):
        for t in tiles:
            right[t][stage].finish()

    def turn(stage, tiles):
        finish(stage, tiles)
        start(stage + 2, tiles)

    def inv_first():
        for ring, _ in inv:
            ring.start()

    def inv_first_forward():
        for ring, _ in inv:
            ring.forward()

    def inv_turn():
        for first_ring, second_ring in inv:
            first_ring.finish()
            second_ring.start()

    def inv_second_forward():
        for _, ring in inv:
            ring.forward()

    def inv_second_finish():
        for _, ring in inv:
            ring.finish()

    def column_chunk(s):
        return pl.ds(pl.multiple_of(128 * s, 128), 128)

    l_ring = Ring(sems, y, yp, ym, lambda s: lbuf.at[p, :, :, column_chunk(s)], lambda s, h: lbuf.at[p, pl.ds(8 * h, 8), :, column_chunk(s)])
    r_ring = Ring(sems, y, yp, ym, lambda s: rj.at[:, :, column_chunk(s)], lambda s, h: rj.at[pl.ds(8 * h, 8), :, column_chunk(s)])
    swaps = {"l": sems.take(4), "w": sems.take(4), "a": sems.take(4)}

    def swap(kind, slot, ref):
        return sems.copy(ref, ref, swaps[kind] + slot, swaps[kind] + slot, mate)

    def left_swap(n, owner):
        s = (l_ring.me, l_ring.left, l_ring.right, l_ring.far)[n]
        return swap("l", n, lbuf.at[owner, :, :, column_chunk(s)])

    def inv_swap(k, owner):
        return swap("a", k, abuf.at[k, pl.ds(k, 4 - k), :, owner])

    def w_swap(k, owner):
        return swap("w", k, wbuf.at[owner, 512 * k:512 * k + 512])

    def compute_s():
        for b in range(4):
            acc = None
            for k in range(b + 1):
                term = jnp.dot(abuf[k, b].reshape(512, 512), rj[4 * k:4 * k + 4].reshape(512, 512), preferred_element_type=F32)
                acc = term if acc is None else acc + term
            sj[b] = acc.astype(BF)

    def compute_w():
        for k in range(4):
            acc = None
            for b in range(k, 4):
                term = dot_tn(abuf[k, b].reshape(512, 512), sj[b])
                acc = term if acc is None else acc + term
            wbuf[p, 512 * k:512 * k + 512] = acc.astype(BF)

    def compute_core(t, n):
        j = p if n == 0 else 1 - p
        k_live = lax.broadcasted_iota(jnp.int32, (512, 512), 1) < rank_ref[4 * row + t]
        l_live = lax.broadcasted_iota(jnp.int32, (512, 512), 0) < rank_ref[2 * col + j]
        acc = dot_tn(wbuf[j], rbuf[t].reshape(2048, 512))
        cores[j, t] = jnp.where(jnp.logical_and(k_live, l_live), acc, 0.0).astype(BF)

    def compute_weight():
        @pl.loop(0, 2)
        def _(j):
            factor = lbuf[j].reshape(2048, 512)
            weight[j] = (dot_tn(factor, factor) * (1.0 / 2048)).astype(BF)

    def compute_gram(t):
        @pl.loop(0, 2)
        def _(j):
            core = cores[j, t]
            half = jnp.dot(weight[j], core, preferred_element_type=F32).astype(BF)
            grams[t, j] = dot_tn(core, half).astype(BF)

    left_copy = pltpu.make_async_copy(lbuf, left_out, local_sem.at[7])

    def l_start():
        l_ring.start()
        left_swap(0, p).start()

    def l_finish():
        l_ring.finish()
        for n in range(1, 4):
            left_swap(n, p).start()

    def l_take():
        for n in range(4):
            left_swap(n, 1 - p).wait_recv()
        left_copy.start()

    def inv_send():
        for k in range(4):
            inv_swap(k, p).start()

    def inv_take():
        for k in range(4):
            inv_swap(k, 1 - p).wait_recv()

    def w_send():
        for k in range(4):
            w_swap(k, p).start()

    def w_take():
        for k in range(4):
            w_swap(k, 1 - p).wait_recv()

    def drain_early():
        for which in range(2):
            drain_pieces(which)
        for rings in inv:
            for ring in rings:
                ring.drain()
        for t in range(4):
            right[t][0].drain()
            right[t][1].drain()
        r_ring.drain()
        for k in range(4):
            inv_swap(k, p).wait_send()
            w_swap(k, p).wait_send()

    def drain_left():
        l_ring.drain()
        for k in range(4):
            left_swap(k, p).wait_send()

    for k in range(4):
        own_inv[k].wait()
    own_right.wait()
    inv_first()
    send_pieces(0)
    start(0, (0, 1))
    inv_first_forward()
    forward(0, (0, 1))
    inv_turn()
    start(1, range(4))
    take_pieces(0)
    r_ring.start()
    turn(0, (0, 1))
    forward(1, range(4))
    r_ring.forward()
    inv_second_forward()
    start(0, (2, 3))
    send_pieces(1)
    forward(2, (0,))
    forward(0, (2, 3))
    inv_second_finish()
    inv_send()
    turn(1, (0,))
    r_ring.finish()
    inv_take()
    compute_s()
    take_pieces(1)
    l_start()
    forward(2, (1,))
    turn(0, (2, 3))
    turn(1, (1,))
    compute_w()
    w_send()
    forward(3, (0,))
    l_ring.forward()
    turn(1, (2,))
    finish(2, (0, 1))
    finish(3, (0,))
    compute_core(0, 0)
    forward(3, (1,))
    w_take()
    compute_core(0, 1)
    forward(2, (2, 3))
    turn(1, (3,))
    l_finish()
    finish(3, (1,))
    compute_core(1, 0)
    compute_core(1, 1)
    drain_early()
    forward(3, (2,))
    l_take()
    compute_weight()
    forward(3, (3,))
    compute_gram(0)
    compute_gram(1)
    drain_left()
    finish(2, (2,))
    finish(3, (2,))
    compute_core(2, 0)
    compute_core(2, 1)
    compute_gram(2)
    finish(2, (3,))
    finish(3, (3,))
    compute_core(3, 0)
    compute_core(3, 1)
    compute_gram(3)
    for t in range(4):
        right[t][2].drain()
        right[t][3].drain()
    left_copy.wait()


def gather(pan_left, pan_right, inverse, rank_list):
    return pl.pallas_call(
        gather_kernel,
        out_shape=(
            pltpu.VMEM((2, 4, 512, 512), BF), pltpu.VMEM((2, 16, 128, 512), BF), pltpu.VMEM((4, 2, 512, 512), BF),
        ),
        in_specs=[pl.BlockSpec(memory_space=pltpu.HBM)] * 3 + [pl.BlockSpec(memory_space=pltpu.SMEM)],
        out_specs=[pl.BlockSpec(memory_space=pltpu.VMEM)] * 3,
        scratch_shapes=[
            pltpu.VMEM((4, 4, 4, 128, 512), BF),
            pltpu.VMEM((4, 4, 4, 2, 64, 512), BF),
            pltpu.VMEM((2, 2048, 512), BF),
            pltpu.VMEM((2, 16, 128, 512), BF),
            pltpu.VMEM((16, 128, 512), BF),
            pltpu.VMEM((4, 512, 512), BF),
            pltpu.VMEM((2, 512, 512), BF),
            pltpu.SemaphoreType.DMA((192,)),
            pltpu.SemaphoreType.DMA((192,)),
            pltpu.SemaphoreType.DMA((8,)),
        ],
        compiler_params=pltpu.CompilerParams(collective_id=0, has_side_effects=True, vmem_limit_bytes=54329344),
        name="gather",
    )(pan_left, pan_right, inverse.reshape(2, 64, 2048), rank_list)


def update_kernel(core_ref, left_ref, gram_in, update_ref, gram_ref):
    j, i = pl.program_id(0), pl.program_id(1)
    update_ref[0, 0] = jnp.dot(left_ref[j].reshape(2048, 512), core_ref[j, i], preferred_element_type=F32).astype(BF)
    gram_ref[0, 0] = gram_in[i, j]


def local(pan_left, pan_right, inverse, rank_list):
    core, left, gram = gather(pan_left, pan_right, inverse, rank_list)
    return pl.pallas_call(
        update_kernel,
        grid=(2, 4),
        out_shape=(jax.ShapeDtypeStruct((4, 2, 2048, 512), BF), jax.ShapeDtypeStruct((4, 2, 512, 512), BF)),
        in_specs=[pl.BlockSpec(memory_space=pltpu.VMEM)] * 3,
        out_specs=(
            pl.BlockSpec((1, 1, 2048, 512), lambda j, i: (i, j, 0, 0)),
            pl.BlockSpec((1, 1, 512, 512), lambda j, i: (i, j, 0, 0)),
        ),
        compiler_params=pltpu.CompilerParams(vmem_limit_bytes=24 << 20),
        name="update",
    )(core, left, gram)


def solution(mesh):
    in_specs = (P("row", "col", None), P("row", "col", None), P("col", None), P())
    out_specs = (P("row", "col", None, None), P("row", "col", None, None))
    return jax.shard_map(local, mesh=mesh, in_specs=in_specs, out_specs=out_specs, check_vma=False)
```

time: 122 us -> 116 us (0.951)
  Pallas kernels: 119 us -> 116 us
  local copies, waits for them, and re-layouts: 2.18 us -> 0 us
    pallas_call x1, Pallas kernels: 21.3 us -> 12.1 us  [local(): pl.pallas_call(update_kernel, grid=(2, 4), out_shape=(jax.ShapeDtypeStruc...]
    pallas_call x1, Pallas kernels: 97.4 us -> 104 us  [gather(): pl.pallas_call(gather_kernel, out_shape=(pltpu.VMEM((2, 4, 512, 512), BF)...]
    unnamed x2 -> x0, local copies, waits for them, and re-layouts: 2.18 us -> none
where the time goes in v2:
time: 116 us
  Pallas kernels  116 us (100%)
    pallas_call x1, Pallas kernels, gather(): pl.pallas_call(gather_kernel, out_shape=(pltpu.VMEM((2, 4, 512, 512), BF)...  104 us
    pallas_call x1, Pallas kernels, local(): pl.pallas_call(update_kernel, grid=(2, 4), out_shape=(jax.ShapeDtypeStruc...  12.1 us

profile of v2, /device:TPU:1, one launch (start us, length us, event | category | flops | bytes accessed | tf_op | source)
XLA Modules:
  0.0 116.2 jit_solution(16253998645887644200)
XLA Ops:
  0.6 103.5 %gather.1 = (bf16[2,4,512,512]{3,2,1,0:T(8,128)(2,1)S(1)}, bf16[2,16,128,512]{3,2,1,0:T(8,128)(2,1)S(1)}, bf16[4,2,512,512]{3,2,1,0:T(8,128)(2,1)S(1)}) custom-call(bf16[4,128,512]{2,1,0:T(8,128)(2,1)} %left_ref.1, bf16[4,128,512]{2,1,0:T(8,128)(2,1)} %right_ref.1, bf16[2,64,2048]{2,1,0:T(8,128)(2,1)} %bitcast.1, s32[32]{0:T(128)} %rank_ref.1), custom_call_target="tpu_custom_call" | custom-call | tf_op jit(solution)/shard_map/gather/pallas_call | solution.py:393
  104.1 12.1 %update.1 = (bf16[4,2,2048,512]{3,2,1,0:T(8,128)(2,1)}, bf16[4,2,512,512]{3,2,1,0:T(8,128)(2,1)}) custom-call(bf16[2,4,512,512]{3,2,1,0:T(8,128)(2,1)S(1)} %get-tuple-element.5.core_ref, bf16[2,16,128,512]{3,2,1,0:T(8,128)(2,1)S(1)} %get-tuple-element.6.left_ref, bf16[4,2,512,512]{3,2,1,0:T(8,128)(2,1)S(1)} %get-tuple-element.7.gram_in), custom_call_target="tpu_custom_call" | custom-call | tf_op jit(solution)/shard_map/update/pallas_call | solution.py:425

commit v3 on v2

--- a/solution.py
+++ b/solution.py
@@ -91,8 +91,8 @@
 
 
 def gather_kernel(
-    left_ref, right_ref, inv_ref, rank_ref, cores, left_out, grams,
-    rbuf, abuf, wbuf, lbuf, rj, sj, weight, send_sem, recv_sem, local_sem,
+    left_ref, right_ref, inv_ref, rank_ref, cores, lbuf, grams,
+    rbuf, abuf, wbuf, rj, sj, weight, send_sem, recv_sem, local_sem,
 ):
     row, col = lax.axis_index("row"), lax.axis_index("col")
     x, z, y, p = lax.rem(col, 4), lax.div(col, 4), lax.div(row, 2), lax.rem(row, 2)
@@ -215,7 +215,7 @@
 
     l_ring = Ring(sems, y, yp, ym, lambda s: lbuf.at[p, :, :, column_chunk(s)], lambda s, h: lbuf.at[p, pl.ds(8 * h, 8), :, column_chunk(s)])
     r_ring = Ring(sems, y, yp, ym, lambda s: rj.at[:, :, column_chunk(s)], lambda s, h: rj.at[pl.ds(8 * h, 8), :, column_chunk(s)])
-    swaps = {"l": sems.take(4), "w": sems.take(4), "a": sems.take(4)}
+    swaps = {"l": sems.take(4), "w": sems.take(4), "a": sems.take(16), "g": sems.take(1)}
 
     def swap(kind, slot, ref):
         return sems.copy(ref, ref, swaps[kind] + slot, swaps[kind] + slot, mate)
@@ -224,8 +224,17 @@
         s = (l_ring.me, l_ring.left, l_ring.right, l_ring.far)[n]
         return swap("l", n, lbuf.at[owner, :, :, column_chunk(s)])
 
-    def inv_swap(k, owner):
-        return swap("a", k, abuf.at[k, pl.ds(k, 4 - k), :, owner])
+    def inv_swap(k, n, owner):
+        slot = lax.rem(x + n, 4)
+        return swap("a", 4 * k + n, abuf.at[k, pl.ds(k, 4 - k), slot, owner])
+
+    def inv_send(*slots):
+        for n in slots:
+            for k in range(4):
+                inv_swap(k, n, p).start()
+
+    def weight_swap(owner):
+        return swap("g", 0, weight.at[owner])
 
     def w_swap(k, owner):
         return swap("w", k, wbuf.at[owner, 512 * k:512 * k + 512])
@@ -254,10 +263,8 @@
         cores[j, t] = jnp.where(jnp.logical_and(k_live, l_live), acc, 0.0).astype(BF)
 
     def compute_weight():
-        @pl.loop(0, 2)
-        def _(j):
-            factor = lbuf[j].reshape(2048, 512)
-            weight[j] = (dot_tn(factor, factor) * (1.0 / 2048)).astype(BF)
+        factor = lbuf[p].reshape(2048, 512)
+        weight[p] = (dot_tn(factor, factor) * (1.0 / 2048)).astype(BF)
 
     def compute_gram(t):
         @pl.loop(0, 2)
@@ -266,8 +273,6 @@
             half = jnp.dot(weight[j], core, preferred_element_type=F32).astype(BF)
             grams[t, j] = dot_tn(core, half).astype(BF)
 
-    left_copy = pltpu.make_async_copy(lbuf, left_out, local_sem.at[7])
-
     def l_start():
         l_ring.start()
         left_swap(0, p).start()
@@ -280,15 +285,11 @@
     def l_take():
         for n in range(4):
             left_swap(n, 1 - p).wait_recv()
-        left_copy.start()
-
-    def inv_send():
-        for k in range(4):
-            inv_swap(k, p).start()
 
     def inv_take():
         for k in range(4):
-            inv_swap(k, 1 - p).wait_recv()
+            for n in range(4):
+                inv_swap(k, n, 1 - p).wait_recv()
 
     def w_send():
         for k in range(4):
@@ -309,10 +310,12 @@
             right[t][1].drain()
         r_ring.drain()
         for k in range(4):
-            inv_swap(k, p).wait_send()
+            for n in range(4):
+                inv_swap(k, n, p).wait_send()
             w_swap(k, p).wait_send()
 
     def drain_left():
+        weight_swap(p).wait_send()
         l_ring.drain()
         for k in range(4):
             left_swap(k, p).wait_send()
@@ -322,71 +325,72 @@
     own_right.wait()
     inv_first()
     send_pieces(0)
-    start(0, (0, 1))
+    send_pieces(1)
+    start(0, range(4))
     inv_first_forward()
-    forward(0, (0, 1))
+    forward(0, range(4))
     inv_turn()
+    inv_send(0)
     start(1, range(4))
     take_pieces(0)
     r_ring.start()
     turn(0, (0, 1))
     forward(1, range(4))
     r_ring.forward()
+    take_pieces(1)
+    l_start()
     inv_second_forward()
-    start(0, (2, 3))
-    send_pieces(1)
-    forward(2, (0,))
-    forward(0, (2, 3))
+    inv_send(1, 3)
+    turn(0, (2,))
+    forward(2, (0, 1))
+    turn(1, (0,))
+    turn(0, (3,))
     inv_second_finish()
-    inv_send()
-    turn(1, (0,))
+    inv_send(2)
+    turn(1, (1, 2))
     r_ring.finish()
     inv_take()
     compute_s()
-    take_pieces(1)
-    l_start()
-    forward(2, (1,))
-    turn(0, (2, 3))
-    turn(1, (1,))
+    forward(2, (2,))
+    forward(3, (0,))
+    turn(1, (3,))
+    l_ring.forward()
     compute_w()
     w_send()
-    forward(3, (0,))
-    l_ring.forward()
-    turn(1, (2,))
     finish(2, (0, 1))
     finish(3, (0,))
+    forward(3, (1,))
     compute_core(0, 0)
-    forward(3, (1,))
     w_take()
     compute_core(0, 1)
-    forward(2, (2, 3))
-    turn(1, (3,))
     l_finish()
+    forward(2, (3,))
+    forward(3, (2,))
     finish(3, (1,))
+    compute_weight()
     compute_core(1, 0)
+    forward(3, (3,))
     compute_core(1, 1)
-    drain_early()
-    forward(3, (2,))
-    l_take()
-    compute_weight()
-    forward(3, (3,))
-    compute_gram(0)
-    compute_gram(1)
-    drain_left()
+    weight_swap(p).start()
     finish(2, (2,))
     finish(3, (2,))
     compute_core(2, 0)
     compute_core(2, 1)
+    weight_swap(1 - p).wait_recv()
+    compute_gram(0)
+    compute_gram(1)
+    drain_early()
     compute_gram(2)
     finish(2, (3,))
     finish(3, (3,))
+    l_take()
+    drain_left()
     compute_core(3, 0)
     compute_core(3, 1)
     compute_gram(3)
     for t in range(4):
         right[t][2].drain()
         right[t][3].drain()
-    left_copy.wait()
 
 
 def gather(pan_left, pan_right, inverse, rank_list):
@@ -401,13 +405,12 @@
             pltpu.VMEM((4, 4, 4, 128, 512), BF),
             pltpu.VMEM((4, 4, 4, 2, 64, 512), BF),
             pltpu.VMEM((2, 2048, 512), BF),
-            pltpu.VMEM((2, 16, 128, 512), BF),
             pltpu.VMEM((16, 128, 512), BF),
             pltpu.VMEM((4, 512, 512), BF),
             pltpu.VMEM((2, 512, 512), BF),
-            pltpu.SemaphoreType.DMA((192,)),
-            pltpu.SemaphoreType.DMA((192,)),
-            pltpu.SemaphoreType.DMA((8,)),
+            pltpu.SemaphoreType.DMA((161,)),
+            pltpu.SemaphoreType.DMA((161,)),
+            pltpu.SemaphoreType.DMA((7,)),
         ],
         compiler_params=pltpu.CompilerParams(collective_id=0, has_side_effects=True, vmem_limit_bytes=54329344),
         name="gather",

time: 116 us -> 105 us (0.905)
  Pallas kernels: 116 us -> 105 us
    pallas_call x1, Pallas kernels: 104 us -> 92.6 us  [gather(): pl.pallas_call(gather_kernel, out_shape=(pltpu.VMEM((2, 4, 512, 512), BF)...]
where the time goes in v3:
time: 105 us
  Pallas kernels  105 us (100%)
    pallas_call x1, Pallas kernels, gather(): pl.pallas_call(gather_kernel, out_shape=(pltpu.VMEM((2, 4, 512, 512), BF)...  92.6 us
    pallas_call x1, Pallas kernels, local(): pl.pallas_call(update_kernel, grid=(2, 4), out_shape=(jax.ShapeDtypeStruc...  12.1 us

profile of v3, /device:TPU:1, one launch (start us, length us, event | category | flops | bytes accessed | tf_op | source)
XLA Modules:
  0.0 105.3 jit_solution(12091425066057706485)
XLA Ops:
  0.6 92.6 %gather.1 = (bf16[2,4,512,512]{3,2,1,0:T(8,128)(2,1)S(1)}, bf16[2,16,128,512]{3,2,1,0:T(8,128)(2,1)S(1)}, bf16[4,2,512,512]{3,2,1,0:T(8,128)(2,1)S(1)}) custom-call(bf16[4,128,512]{2,1,0:T(8,128)(2,1)} %left_ref.1, bf16[4,128,512]{2,1,0:T(8,128)(2,1)} %right_ref.1, bf16[2,64,2048]{2,1,0:T(8,128)(2,1)} %bitcast.1, s32[32]{0:T(128)} %rank_ref.1), custom_call_target="tpu_custom_call" | custom-call | tf_op jit(solution)/shard_map/gather/pallas_call | solution.py:397
  93.2 12.1 %update.1 = (bf16[4,2,2048,512]{3,2,1,0:T(8,128)(2,1)}, bf16[4,2,512,512]{3,2,1,0:T(8,128)(2,1)}) custom-call(bf16[2,4,512,512]{3,2,1,0:T(8,128)(2,1)S(1)} %get-tuple-element.5.core_ref, bf16[2,16,128,512]{3,2,1,0:T(8,128)(2,1)S(1)} %get-tuple-element.6.left_ref, bf16[4,2,512,512]{3,2,1,0:T(8,128)(2,1)S(1)} %get-tuple-element.7.gram_in), custom_call_target="tpu_custom_call" | custom-call | tf_op jit(solution)/shard_map/update/pallas_call | solution.py:428

commit v4 on v3

--- a/solution.py
+++ b/solution.py
@@ -334,44 +334,48 @@
     start(1, range(4))
     take_pieces(0)
     r_ring.start()
-    turn(0, (0, 1))
+    turn(0, (0,))
     forward(1, range(4))
+    turn(0, (1,))
     r_ring.forward()
     take_pieces(1)
     l_start()
     inv_second_forward()
     inv_send(1, 3)
+    forward(2, (0,))
     turn(0, (2,))
-    forward(2, (0, 1))
     turn(1, (0,))
+    forward(2, (1,))
     turn(0, (3,))
     inv_second_finish()
     inv_send(2)
-    turn(1, (1, 2))
+    turn(1, (1,))
     r_ring.finish()
     inv_take()
     compute_s()
+    forward(3, (0,))
+    turn(1, (2,))
+    compute_w()
+    w_send()
     forward(2, (2,))
-    forward(3, (0,))
     turn(1, (3,))
     l_ring.forward()
-    compute_w()
-    w_send()
-    finish(2, (0, 1))
+    finish(2, (0,))
     finish(3, (0,))
     forward(3, (1,))
     compute_core(0, 0)
     w_take()
     compute_core(0, 1)
     l_finish()
+    compute_weight()
     forward(2, (3,))
     forward(3, (2,))
+    finish(2, (1,))
     finish(3, (1,))
-    compute_weight()
     compute_core(1, 0)
     forward(3, (3,))
+    weight_swap(p).start()
     compute_core(1, 1)
-    weight_swap(p).start()
     finish(2, (2,))
     finish(3, (2,))
     compute_core(2, 0)

time: 105 us -> 105 us (level)
  no operation moved by 1% of the time
where the time goes in v4:
time: 105 us
  Pallas kernels  104 us (99%)
    pallas_call x1, Pallas kernels, gather(): pl.pallas_call(gather_kernel, out_shape=(pltpu.VMEM((2, 4, 512, 512), BF)...  91.8 us
    pallas_call x1, Pallas kernels, local(): pl.pallas_call(update_kernel, grid=(2, 4), out_shape=(jax.ShapeDtypeStruc...  12.1 us

profile of v4, /device:TPU:1, one launch (start us, length us, event | category | flops | bytes accessed | tf_op | source)
XLA Modules:
  0.0 104.5 jit_solution(9236681780408316697)
XLA Ops:
  0.6 91.8 %gather.1 = (bf16[2,4,512,512]{3,2,1,0:T(8,128)(2,1)S(1)}, bf16[2,16,128,512]{3,2,1,0:T(8,128)(2,1)S(1)}, bf16[4,2,512,512]{3,2,1,0:T(8,128)(2,1)S(1)}) custom-call(bf16[4,128,512]{2,1,0:T(8,128)(2,1)} %left_ref.1, bf16[4,128,512]{2,1,0:T(8,128)(2,1)} %right_ref.1, bf16[2,64,2048]{2,1,0:T(8,128)(2,1)} %bitcast.1, s32[32]{0:T(128)} %rank_ref.1), custom_call_target="tpu_custom_call" | custom-call | tf_op jit(solution)/shard_map/gather/pallas_call | solution.py:401
  92.5 12.1 %update.1 = (bf16[4,2,2048,512]{3,2,1,0:T(8,128)(2,1)}, bf16[4,2,512,512]{3,2,1,0:T(8,128)(2,1)}) custom-call(bf16[2,4,512,512]{3,2,1,0:T(8,128)(2,1)S(1)} %get-tuple-element.5.core_ref, bf16[2,16,128,512]{3,2,1,0:T(8,128)(2,1)S(1)} %get-tuple-element.6.left_ref, bf16[4,2,512,512]{3,2,1,0:T(8,128)(2,1)S(1)} %get-tuple-element.7.gram_in), custom_call_target="tpu_custom_call" | custom-call | tf_op jit(solution)/shard_map/update/pallas_call | solution.py:432
